TPU v7x, 256 devices: a whole 4x4x8 slice. The times are simulated.
256 devices in a mesh: req: 16 (over y_hi, x, core), tp: 16 (over y_lo, z).
Axes of the slice: x: 4, y: 4 (y_hi: 2, y_lo: 2; y = y_hi * 2 + y_lo), z: 8, core: 2. Of those that a mesh axis runs over, the one named last changes fastest.
Arguments:
- tokens: bfloat16 [14336, 5120], P(('req', 'tp')), may hold values from -6 to 6
- qkv_weight: bfloat16 [5120, 3, 4096], P('req', None, 'tp')
- out_weight: bfloat16 [4096, 5120], P('tp', 'req')
- query_key_gain: float32 [2, 4096], P(None, 'tp'), may hold values from 0.25 to 1.75
- post_gain: float32 [5120], replicated, may hold values from 0.25 to 1.75
- pool_cache: bfloat16 [512, 128, 2, 4096], P('req', None, None, 'tp'), may hold values from -68 to 68
- lengths: int32 [16, 16], P('req'), may hold values from 1 to 256, 896 in all within a row
- prefix_pages: int32 [16, 16], P('req'), may hold values from 1 to 16, 32 in all within a row
- pool_order: int32 [16, 32], P('req'), may hold values from 0 to 31, each once within a row
- owners: int32 [16, 16], P('req'), may hold values from 0 to 15, each once within a row
Outputs:
- hidden: bfloat16 [14336, 5120], P(('req', 'tp'))
- handed_pages: bfloat16 [512, 128, 2, 4096], P('req', None, None, 'tp')
Inputs may be any that keep to these rules, and one draw needn't show every extreme that they name: `lengths`: each row sums to 896; the largest entry of every row is exactly 256. `prefix_pages`: each row sums to 32; the largest entry of every row is exactly 16. `pool_order`: each row names every slot once. `owners`: each row names every owner once.
All inputs are finite; a program needn't handle non-finite values.
Results may differ from a plain program's by a relative error of at most 0.014.
Values may be sent and summed in bfloat16 or wider, within the bound.
A program may use at most 128 MiB of HBM per device.

v0:
```python
import jax
import jax.numpy as jnp
from jax import lax
from jax.sharding import PartitionSpec as P

HEADS = 32
HEAD = 128
PAGE = 128
CAP = 2


norm_eps = 1e-06
rope_base = 500000.0
masked_score = -1e30


def token_layout(lengths_row, prefix_row, block_len):
    ends_at = jnp.cumsum(lengths_row)
    starts_at = ends_at - lengths_row
    token_ids = jnp.arange(block_len, dtype=jnp.int32)
    request_of = jnp.sum((token_ids[:, None] >= ends_at[None, :]).astype(jnp.int32), axis=1)
    one_hot = (
        request_of[:, None] == jnp.arange(lengths_row.shape[0], dtype=jnp.int32)[None, :]
    ).astype(jnp.int32)
    shift_of = jnp.sum(one_hot * (prefix_row * PAGE - starts_at)[None, :], axis=1)
    return (request_of, token_ids + shift_of, starts_at)


def slot_owner(prefix_row, order_row):
    page_ends = jnp.cumsum(prefix_row)
    page_ids = jnp.arange(order_row.shape[0], dtype=jnp.int32)
    page_request = jnp.sum((page_ids[:, None] >= page_ends[None, :]).astype(jnp.int32), axis=1)
    matches = (order_row[None, :] == page_ids[:, None]).astype(jnp.int32)
    return jnp.sum(matches * page_request[None, :], axis=1)


def rotate_heads(tensor, positions):
    half_dim = HEAD // 2
    frequency = rope_base ** (-(2.0 * jnp.arange(half_dim, dtype=jnp.float32)) / HEAD)
    angles = positions.astype(jnp.float32)[:, None] * frequency[None, :]
    cosine = jnp.cos(angles)[:, None, :]
    sine_part = jnp.sin(angles)[:, None, :]
    first_half = tensor[..., :half_dim]
    second_half = tensor[..., half_dim:]
    return jnp.concatenate(
        [
            first_half * cosine - second_half * sine_part,
            second_half * cosine + first_half * sine_part,
        ],
        axis=-1,
    )


def attend_head(queries, pool_keys, pool_values, new_keys, new_values, pool_mask, block_mask):
    score_scale = HEAD ** (-0.5)
    pool_scores = jnp.dot(queries, pool_keys.T, preferred_element_type=jnp.float32) * score_scale
    block_scores = jnp.dot(queries, new_keys.T, preferred_element_type=jnp.float32) * score_scale
    pool_scores = jnp.where(pool_mask, pool_scores, masked_score)
    block_scores = jnp.where(block_mask, block_scores, masked_score)
    row_max = jnp.maximum(jnp.max(pool_scores, axis=1), jnp.max(block_scores, axis=1))
    pool_exp = jnp.exp(pool_scores - row_max[:, None])
    block_exp = jnp.exp(block_scores - row_max[:, None])
    row_total = jnp.sum(pool_exp, axis=1) + jnp.sum(block_exp, axis=1)
    pool_weights = (pool_exp / row_total[:, None]).astype(jnp.bfloat16)
    block_weights = (block_exp / row_total[:, None]).astype(jnp.bfloat16)
    mixed_out = jnp.dot(pool_weights, pool_values, preferred_element_type=jnp.float32)
    mixed_out = mixed_out + jnp.dot(block_weights, new_values, preferred_element_type=jnp.float32)
    return mixed_out.astype(jnp.bfloat16)


def build_send(kv_new, lengths_row, starts_at, owner_row):
    page_span = CAP * PAGE
    owner_count = owner_row.shape[0]
    owner_ids = jnp.arange(owner_count, dtype=jnp.int32)
    owner_pick = (owner_row[None, :] == owner_ids[:, None]).astype(jnp.int32)
    start_of = jnp.sum(owner_pick * starts_at[None, :], axis=1)
    length_of = jnp.sum(owner_pick * lengths_row[None, :], axis=1)
    offsets = jnp.arange(page_span, dtype=jnp.int32)
    source = start_of[:, None] + offsets[None, :]
    is_valid = offsets[None, :] < length_of[:, None]
    source = jnp.clip(source, 0, kv_new.shape[0] - 1).reshape(-1)
    taken_rows = jnp.take(kv_new, source, axis=0).reshape(
        owner_count, page_span, kv_new.shape[1], kv_new.shape[2]
    )
    return jnp.where(is_valid[:, :, None, None], taken_rows, jnp.zeros_like(taken_rows))


def hand_over(kv_new, lengths_row, starts_at, owner_row):
    outgoing = build_send(kv_new, lengths_row, starts_at, owner_row)
    arrived = lax.all_to_all(outgoing, "req", split_axis=0, concat_axis=0, tiled=True)
    return arrived.reshape(arrived.shape[0] * CAP, PAGE, arrived.shape[2], arrived.shape[3])


def body(
    tokens,
    qkv_weight,
    out_weight,
    query_key_gain,
    post_gain,
    pool_cache,
    lengths,
    prefix_pages,
    pool_order,
    owners,
):
    local_width = qkv_weight.shape[2]
    heads_here = local_width // HEAD
    block_tokens = lax.all_gather(tokens, "tp", axis=0, tiled=True)
    block_len = block_tokens.shape[0]
    row_piece = lax.all_gather(qkv_weight, "req", axis=0, tiled=True)
    flat_piece = row_piece.reshape(row_piece.shape[0], 3 * local_width)
    joined_all = jnp.dot(block_tokens, flat_piece, preferred_element_type=jnp.float32)
    joined_all = joined_all.reshape(block_len, 3, local_width)
    queries = joined_all[:, 0]
    keys_raw = joined_all[:, 1]
    values_raw = joined_all[:, 2]
    local_sums = jnp.stack(
        [jnp.sum(queries * queries, axis=1), jnp.sum(keys_raw * keys_raw, axis=1)]
    )
    global_sums = lax.psum(local_sums, "tp")
    inverse = lax.rsqrt(global_sums / (HEADS * HEAD) + norm_eps)
    queries = queries * inverse[0][:, None] * query_key_gain[0]
    keys_raw = keys_raw * inverse[1][:, None] * query_key_gain[1]
    lengths_row = lengths[0]
    prefix_row = prefix_pages[0]
    request_of, positions, starts_at = token_layout(lengths_row, prefix_row, block_len)
    query_rot = rotate_heads(queries.reshape(block_len, heads_here, HEAD), positions).astype(
        jnp.bfloat16
    )
    key_rot = rotate_heads(keys_raw.reshape(block_len, heads_here, HEAD), positions).astype(
        jnp.bfloat16
    )
    value_new = values_raw.reshape(block_len, heads_here, HEAD).astype(jnp.bfloat16)
    kv_new = jnp.stack(
        [key_rot.reshape(block_len, local_width), value_new.reshape(block_len, local_width)], axis=1
    )
    pool_count = pool_cache.shape[0]
    key_owner = jnp.repeat(slot_owner(prefix_row, pool_order[0]), PAGE)
    pool_mask = request_of[:, None] == key_owner[None, :]
    token_ids = jnp.arange(block_len, dtype=jnp.int32)
    block_mask = (request_of[:, None] == request_of[None, :]) & (
        token_ids[None, :] <= token_ids[:, None]
    )
    pool_keys = pool_cache[:, :, 0, :].reshape(pool_count * PAGE, heads_here, HEAD)
    pool_values = pool_cache[:, :, 1, :].reshape(pool_count * PAGE, heads_here, HEAD)
    head_outs = lax.map(
        lambda per_head: attend_head(
            per_head[0], per_head[1], per_head[2], per_head[3], per_head[4], pool_mask, block_mask
        ),
        (
            jnp.moveaxis(query_rot, 1, 0),
            jnp.moveaxis(pool_keys, 1, 0),
            jnp.moveaxis(pool_values, 1, 0),
            jnp.moveaxis(key_rot, 1, 0),
            jnp.moveaxis(value_new, 1, 0),
        ),
    )
    attention = jnp.moveaxis(head_outs, 0, 1).reshape(block_len, local_width)
    out_full = lax.all_gather(out_weight, "req", axis=1, tiled=True)
    projected = lax.psum_scatter(
        jnp.dot(attention, out_full, preferred_element_type=jnp.float32).astype(jnp.bfloat16),
        "tp",
        scatter_dimension=0,
        tiled=True,
    ).astype(jnp.float32)
    post_scale = lax.rsqrt(jnp.mean(projected * projected, axis=1, keepdims=True) + norm_eps)
    hidden = (tokens.astype(jnp.float32) + projected * post_scale * post_gain[None, :]).astype(
        jnp.bfloat16
    )
    handed_pages = hand_over(kv_new, lengths_row, starts_at, owners[0])
    return (hidden, handed_pages)


def solution(mesh):
    in_specs = (
        P(("req", "tp"), None),
        P("req", None, "tp"),
        P("tp", "req"),
        P(None, "tp"),
        P(),
        P("req", None, None, "tp"),
        P("req", None),
        P("req", None),
        P("req", None),
        P("req", None),
    )
    out_specs = (P(("req", "tp"), None), P("req", None, None, "tp"))
    return jax.shard_map(body, mesh=mesh, in_specs=in_specs, out_specs=out_specs, check_vma=False)
```

profile of v0, /device:TPU:1, one launch (start us, length us, event | category | flops | bytes accessed | tf_op | source)
XLA Modules:
  0.0 490.6 jit_solution(5319571095638446805)
XLA Ops:
  7.2 0.7 all-gather.6.cloned.1.call-update
  7.9 0.7 all-gather.4.cloned.1.call-update
  8.7 0.7 all-gather.8.cloned.1.call-update
  9.5 0.8 fusion.45
  10.2 0.7 copy.47
  11.2 1.2 fusion.43
  12.5 21.7 %slice_reduce_fusion = (bf16[32,128,256]{2,1,0:T(8,128)(2,1)}, bf16[32,128,256]{2,1,0:T(8,128)(2,1)}) fusion(bf16[32,128,2,256]{3,2,1,0:T(2,128)(2,1)} %param.17), kind=kLoop, calls=%fused_computation.45 | loop fusion | bytes 8388608 | tf_op jit(solution)/shard_map/slice | solution.py:145
  34.2 2.6 reshape.260
  36.8 4.0 reshape.259
  41.2 1.7 multiply_cosine_fusion
  42.9 4.2 copy_bitcast_fusion
  47.1 43.6 %all-gather.6.cloned.1.call-done = bf16[5120,3,256]{2,0,1:T(8,128)(2,1)} async-done(((bf16[320,3,256]{2,0,1:T(8,128)(2,1)}), bf16[5120,3,256]{2,0,1:T(8,128)(2,1)}) %all-gather.6.cloned.1.call-update) | async-done | bytes 7864336 | tf_op jit(solution)/shard_map/all_gather | solution.py:110
  90.7 10.8 %copy.45 = bf16[5120,3,256]{0,2,1:T(8,128)(2,1)} copy(bf16[5120,3,256]{2,0,1:T(8,128)(2,1)} %all-gather.6.cloned.1.call-done) | data formatting | bytes 15728640 | tf_op jit(solution)/shard_map/all_gather | solution.py:110
  101.5 97.2 %all-gather.4.cloned.1.call-done = bf16[896,5120]{1,0:T(8,128)(2,1)} async-done(((bf16[56,5120]{1,0:T(8,128)(2,1)}), bf16[896,5120]{1,0:T(8,128)(2,1)}) %all-gather.4.cloned.1.call-update) | async-done | bytes 9175056 | tf_op jit(solution)/shard_map/all_gather | solution.py:108
  198.6 12.0 %fusion.32 = f32[896,3,256]{0,2,1:T(8,128)S(1)} fusion(bf16[896,5120]{1,0:T(8,128)(2,1)} %all-gather.4.cloned.1.call-done, bf16[5120,3,256]{0,2,1:T(8,128)(2,1)} %copy.45), kind=kOutput, calls=%fused_computation.39 | convolution fusion | flops 7046430720 | bytes 19791872 | tf_op jit(solution)/shard_map/dot_general | solution.py:112
  210.7 1.1 multiply_reduce_fusion.1
  211.8 2.6 copy.49
  214.5 26.2 %psum.7 = f32[2,896]{1,0:T(2,128)S(1)} all-reduce(f32[2,896]{1,0:T(2,128)S(1)} %pad_maximum_fusion.1), channel_id=1, replica_groups=mesh['req'=16,'tp'=16] {'tp'}, use_global_device_ids=true, to_apply=%region_2.0 | all-reduce | flops 1792 | bytes 14336 | tf_op jit(solution)/shard_map/psum | solution.py:120
  240.7 1.2 copy.46
  242.0 1.8 multiply_multiply_fusion
  243.8 0.4 subtract_convert_fusion
  244.2 0.4 multiply_subtract_fusion
  244.7 0.3 copy.51
  244.9 1.0 maximum_bitcast_fusion
  246.2 59.5 %while.12 = (s32[]{:T(128)}, bf16[2,896,128]{1,2,0:T(8,128)(2,1)}, bf16[2,896,128]{2,1,0:T(8,128)(2,1)}, bf16[2,4096,128]{2,1,0:T(8,128)(2,1)}, bf16[2,896,128]{...) while((s32[]{:T(128)}, bf16[2,896,128]{1,2,0:T(8,128)(2,1)}, ...), condition=%wide.region_14.15_spmd.clone.clone, body=%wide.region_9.14_spmd.clone.clone.sunk | while | flops 2354198784 | bytes 70941888 | solution.py:146
  246.2 9.2 %fusion.59 = (f32[896]{0:T(1024)S(1)}, f32[896,4096]{1,0:T(8,128)}) fusion(s32[4096]{0:T(1024)S(1)} %get-tuple-element.264, s32[896]{0:T(1024)S(1)} %get-tuple-element.265, bf16[2,4096,128]{2,1,0:T(8,128)(2,1)} %get-tuple-element.260, s32[]{:T(128)S(6)} %copy.72, bf16[2,896,128]{2,1,0:T(8,128)(2,1)} %get-tuple-element.259), kind=kOutput, calls=%fused_computation.7.clone.1 | convolution fusion | flops 954203264 | bytes 15982592 | tf_op jit(solution)/shard_map/while/body/eval_jaxpr/dot_general | solution.py:56
  255.5 1.6 fusion.60
  257.1 8.8 %fusion.61 = f32[896]{0:T(1024)S(1)} fusion(f32[896,4096]{1,0:T(8,128)} %get-tuple-element.233, s32[4096]{0:T(1024)S(1)} %get-tuple-element.264, f32[896]{0:T(1024)S(1)} %max.23, s32[896]{0:T(1024)S(1)} %get-tuple-element.265), kind=kLoop, calls=%fused_computation.6.clone.1 | loop fusion | flops 18349184 | bytes 14707200 | tf_op jit(solution)/shard_map/while/body/eval_jaxpr/reduce_sum | solution.py:63
  265.9 0.5 fusion.62
  266.4 7.7 %fusion.63 = f32[896,128]{1,0:T(8,128)S(1)} fusion(f32[896,4096]{1,0:T(8,128)} %get-tuple-element.233, s32[4096]{0:T(1024)S(1)} %get-tuple-element.264, f32[896]{0:T(1024)S(1)} %add.169, f32[896]{0:T(1024)S(1)} %max.23, s32[896]{0:T(1024)S(1)} %get-tuple-element.265, bf16[2,4096,128]{2,1,0:T(8,128)(2,1)S(1)} %copy-done.7, s32[]{:T(128)S(6)} %copy.72), kind=kOutput, calls=%fused_computation.8.clone.1 | convolution fusion | flops 961544192 | bytes 16216068 | tf_op jit(solution)/shard_map/while/body/eval_jaxpr/dot_general | solution.py:66
  274.2 0.7 fusion.64
  275.2 0.8 copy-done.9
  276.0 9.2 %fusion.59 = (f32[896]{0:T(1024)S(1)}, f32[896,4096]{1,0:T(8,128)}) fusion(s32[4096]{0:T(1024)S(1)} %get-tuple-element.264, s32[896]{0:T(1024)S(1)} %get-tuple-element.265, bf16[2,4096,128]{2,1,0:T(8,128)(2,1)} %get-tuple-element.260, s32[]{:T(128)S(6)} %copy.72, bf16[2,896,128]{2,1,0:T(8,128)(2,1)} %get-tuple-element.259), kind=kOutput, calls=%fused_computation.7.clone.1 | convolution fusion | flops 954203264 | bytes 15982592 | tf_op jit(solution)/shard_map/while/body/eval_jaxpr/dot_general | solution.py:56
  285.2 1.6 fusion.60
  286.8 8.8 %fusion.61 = f32[896]{0:T(1024)S(1)} fusion(f32[896,4096]{1,0:T(8,128)} %get-tuple-element.233, s32[4096]{0:T(1024)S(1)} %get-tuple-element.264, f32[896]{0:T(1024)S(1)} %max.23, s32[896]{0:T(1024)S(1)} %get-tuple-element.265), kind=kLoop, calls=%fused_computation.6.clone.1 | loop fusion | flops 18349184 | bytes 14707200 | tf_op jit(solution)/shard_map/while/body/eval_jaxpr/reduce_sum | solution.py:63
  295.6 0.5 fusion.62
  296.1 7.7 %fusion.63 = f32[896,128]{1,0:T(8,128)S(1)} fusion(f32[896,4096]{1,0:T(8,128)} %get-tuple-element.233, s32[4096]{0:T(1024)S(1)} %get-tuple-element.264, f32[896]{0:T(1024)S(1)} %add.169, f32[896]{0:T(1024)S(1)} %max.23, s32[896]{0:T(1024)S(1)} %get-tuple-element.265, bf16[2,4096,128]{2,1,0:T(8,128)(2,1)S(1)} %copy-done.7, s32[]{:T(128)S(6)} %copy.72), kind=kOutput, calls=%fused_computation.8.clone.1 | convolution fusion | flops 961544192 | bytes 16216068 | tf_op jit(solution)/shard_map/while/body/eval_jaxpr/dot_general | solution.py:66
  303.9 0.7 fusion.64
  305.0 0.8 copy-done.9
  305.7 8.0 %convolution_convert_fusion = bf16[896,5120]{1,0:T(8,128)(2,1)} fusion(bf16[896,256]{0,1:T(8,128)(2,1)} %bitcast.104, bf16[256,5120]{0,1:T(8,128)(2,1)} %all-gather.8.cloned.1.call-done), kind=kOutput, calls=%fused_computation.41 | convolution fusion | flops 2353397760 | bytes 12255232 | tf_op jit(solution)/shard_map/dot_general | solution.py:161
  313.8 0.6 copy-done.11
  315.6 1.3 copy.57
  316.8 32.4 %gather_fusion = bf16[4096,2,256]{2,1,0:T(2,128)(2,1)} fusion(bf16[896,2,256]{2,1,0:T(2,128)(2,1)S(1)} %copy.57, s32[4096]{0:T(1024)S(1)} %broadcast_clamp_fusion), kind=kCustom, calls=%fused_computation | custom fusion | bytes 8404992 | tf_op jit(solution)/shard_map/jit(_take)/gather | solution.py:82
  349.3 12.7 %broadcast_select_fusion.1 = bf16[16,256,2,256]{3,2,1,0:T(2,128)(2,1)S(1)} fusion(pred[16,256]{1,0:T(8,128)(4,1)S(1)} %get-tuple-element.172, bf16[16,256,2,256]{3,2,1,0:T(2,128)(2,1)} %bitcast.98, pred[16,256]{1,0:T(8,128)(4,1)S(1)} %get-tuple-element.173), kind=kLoop, calls=%fused_computation.43 | loop fusion | flops 4194304 | bytes 8396800 | tf_op jit(solution)/shard_map/jit(_where)/select_n | solution.py:85
  362.0 109.4 %all_to_all.5 = bf16[16,256,2,256]{3,2,1,0:T(2,128)(2,1)} all-to-all(bf16[16,256,2,256]{3,2,1,0:T(2,128)(2,1)S(1)} %broadcast_select_fusion.1), channel_id=1, replica_groups=mesh['req'=16,'tp'=16] {'req'}, dimensions={0} | all-to-all | bytes 8388608 | tf_op jit(solution)/shard_map/all_to_all | solution.py:90
  471.4 1.3 fusion.35
  472.7 2.1 fusion.38
  474.8 9.2 %copy.79 = bf16[32,128,2,256]{3,2,1,0:T(2,128)(2,1)} copy(bf16[32,128,2,256]{3,2,1,0:T(2,128)(2,1)} %bitcast.99) | data formatting | bytes 8388608
  (80 shorter events, 3.2 us)
Async XLA Ops:
  7.2 83.5 %all-gather.6.cloned.1.call-start = ((), (), s32[]{:S(2)}) async-start(), calls=%async_computation.3 | async-start | bytes 8355840 | tf_op jit(solution)/shard_map/all_gather | solution.py:110
  7.9 190.7 %all-gather.4.cloned.1.call-start = ((), (), s32[]{:S(2)}) async-start(), calls=%async_computation.2 | async-start | bytes 9748480 | tf_op jit(solution)/shard_map/all_gather | solution.py:108
  8.6 297.1 %all-gather.8.cloned.1.call-start = ((), (), s32[]{:S(2)}) async-start(), calls=%async_computation.4 | async-start | bytes 2785280 | tf_op jit(solution)/shard_map/all_gather | solution.py:159
  9.4 462.0 %reduce-scatter.2.cloned.1.call-start = ((), (), s32[]{:S(2)}) async-start(), calls=%async_computation.5 | async-start | bytes 9748480 | tf_op jit(solution)/shard_map/reduce_scatter | solution.py:160
  34.2 6.5 %copy-start.12 = (s32[1,16]{1,0:T(1,128)S(1)}, s32[1,16]{1,0:T(1,128)}, u32[]{:S(2)}) copy-start(s32[1,16]{1,0:T(1,128)} %param.19) | copy-start | bytes 196
  34.2 6.9 %copy-start.15 = (s32[1,32]{1,0:T(1,128)S(1)}, s32[1,32]{1,0:T(1,128)}, u32[]{:S(2)}) copy-start(s32[1,32]{1,0:T(1,128)} %param.20) | copy-start | bytes 388
  211.8 32.8 %copy-start = (bf16[896,1,256]{0,2,1:T(8,128)(2,1)}, bf16[896,1,256]{0,2,1:T(8,128)(2,1)S(1)}, u32[]{:S(2)}) copy-start(bf16[896,1,256]{0,2,1:T(8,128)(2,1)S(1)} %slice.78) | copy-start | bytes 1376260
  244.6 1.6 copy-start.2
  244.6 1.6 copy-start.4
  257.1 9.3 %copy-start.7 = (bf16[2,4096,128]{2,1,0:T(8,128)(2,1)S(1)}, bf16[2,4096,128]{2,1,0:T(8,128)(2,1)}, u32[]{:S(2)}) copy-start(bf16[2,4096,128]{2,1,0:T(8,128)(2,1)} %get-tuple-element.262) | copy-start | bytes 6291460 | tf_op jit(solution)/shard_map/while
  274.2 1.0 copy-start.8
  275.2 0.8 copy-start.9
  286.8 9.3 %copy-start.7 = (bf16[2,4096,128]{2,1,0:T(8,128)(2,1)S(1)}, bf16[2,4096,128]{2,1,0:T(8,128)(2,1)}, u32[]{:S(2)}) copy-start(bf16[2,4096,128]{2,1,0:T(8,128)(2,1)} %get-tuple-element.262) | copy-start | bytes 6291460 | tf_op jit(solution)/shard_map/while
  303.9 1.0 copy-start.8
  304.9 0.8 copy-start.9
  313.7 0.7 copy-start.11
  313.7 0.7 copy-start.13
  313.7 0.7 copy-start.14
  313.7 1.0 copy-start.3
  313.8 1.2 copy-start.5
  313.8 1.7 copy-start.1
  361.9 110.8 %copy-start.6 = (bf16[56,5120]{1,0:T(8,128)(2,1)S(1)}, bf16[56,5120]{1,0:T(8,128)(2,1)}, u32[]{:S(2)}) copy-start(bf16[56,5120]{1,0:T(8,128)(2,1)} %param.12) | copy-start | bytes 1720324
  361.9 110.8 %copy-start.10 = (f32[5120]{0:T(1024)S(1)}, f32[5120]{0:T(1024)}, u32[]{:S(2)}) copy-start(f32[5120]{0:T(1024)} %param.16) | copy-start | bytes 61444
Sparse Core Ops, SparseCore 0:
  10.7 79.8 all-gather.5
  92.4 106.1 all-gather.3
  201.4 53.6 all-gather.7
  313.9 145.5 reduce-scatter.1
where the time goes:
time: 492 us; the launch traced here: 491 us
  waiting for transfers between devices  143 us (29%)
  blocking collectives  136 us (28%)
  local copies, waits for them, and re-layouts  95.2 us (19%)
  matrix products  58.6 us (12%)
  other arithmetic  43.9 us (9%)
  between operations  14 us (3%)
    all_to_all x1, blocking collectives, hand_over(): lax.all_to_all(outgoing, 'req', split_axis=0, concat_axis=0, tiled=True)  109 us
    all_gather x1, waiting for transfers between devices, body(): block_tokens = lax.all_gather(tokens, 'tp', axis=0, tiled=True)  97.2 us
    all_gather x1, waiting for transfers between devices, body(): row_piece = lax.all_gather(qkv_weight, 'req', axis=0, tiled=True)  43.6 us
    gather x1, local copies, waits for them, and re-layouts, build_send(): jnp.take(kv_new, source, axis=0)  32.4 us
    psum x1, blocking collectives, body(): global_sums = lax.psum(local_sums, 'tp')  26.2 us
    slice x1, local copies, waits for them, and re-layouts, body(): pool_cache[:, :, 1, :].reshape(pool_count * PAGE, heads_here, HEAD)  21.7 us
    reduce_sum x4, other arithmetic, attend_head(): row_total = jnp.sum(pool_exp, axis=1) + jnp.sum(block_exp, axis=1)  18.6 us
    dot_general x2, matrix products, attend_head(): jnp.dot(queries, pool_keys.T, preferred_element_type=jnp.float32)  18.5 us
  transfers between devices with their start and end apart: 4, of which 2 were waited for; matrix products, arithmetic and copies ran while one was open for 36% of the time, Pallas kernels for 0%

commit v1 on v0

--- a/solution.py
+++ b/solution.py
@@ -1,6 +1,8 @@
 import jax
 import jax.numpy as jnp
 from jax import lax
+from jax.experimental import pallas as pl
+from jax.experimental.pallas import tpu as pltpu
 from jax.sharding import PartitionSpec as P
 
 HEADS = 32
@@ -12,6 +14,160 @@
 norm_eps = 1e-06
 rope_base = 500000.0
 masked_score = -1e30
+
+
+MESH = pl.DeviceIdType.MESH
+ZN = 8
+SPLIT = 32
+
+
+def ring_place():
+    tp = lax.axis_index("tp")
+    sense = 1 - 2 * lax.rem(lax.axis_index("req"), 2)
+    column = tp // ZN
+    z = lax.rem(tp, ZN)
+
+    def at(col, steps):
+        return col * ZN + lax.rem(z + sense * steps + 4 * ZN, ZN)
+
+    return tp, column, at
+
+
+def greet(peers):
+    barrier = pltpu.get_barrier_semaphore()
+    for peer in peers:
+        pl.semaphore_signal(barrier, inc=1, device_id={"tp": peer}, device_id_type=MESH)
+    pl.semaphore_wait(barrier, len(peers))
+
+
+def gather_kernel(tok_ref, out_ref, local_sem, send_sem, recv_sem):
+    tp, col, at = ring_place()
+    other = 1 - col
+    right, left, across = at(col, 1), at(col, -1), at(other, 0)
+    greet((right, left, across))
+    rows = tok_ref.shape[0]
+    head, tail, full = pl.ds(0, SPLIT), pl.ds(SPLIT, rows - SPLIT), pl.ds(0, rows)
+    sends = []
+
+    def push(src, origin, part, peer, slot):
+        copy = pltpu.make_async_remote_copy(
+            src_ref=src.at[part],
+            dst_ref=out_ref.at[origin, part],
+            send_sem=send_sem.at[slot],
+            recv_sem=recv_sem.at[slot],
+            device_id={"tp": peer},
+            device_id_type=MESH,
+        )
+        copy.start()
+        sends.append(copy)
+
+    def arrive(origin, part, slot):
+        pltpu.make_async_remote_copy(
+            src_ref=out_ref.at[origin, part],
+            dst_ref=out_ref.at[origin, part],
+            send_sem=send_sem.at[slot],
+            recv_sem=recv_sem.at[slot],
+            device_id={"tp": across},
+            device_id_type=MESH,
+        ).wait_recv()
+
+    push(tok_ref, tp, tail, across, 14)
+    push(tok_ref, tp, full, right, 0)
+    push(tok_ref, tp, full, left, 4)
+    push(tok_ref, tp, head, across, 15)
+    keep = pltpu.make_async_copy(tok_ref, out_ref.at[tp], local_sem)
+    keep.start()
+    arrive(across, tail, 14)
+    push(out_ref.at[across], across, tail, right, 7)
+    push(out_ref.at[across], across, tail, left, 11)
+    for k in range(1, 5):
+        origin = at(col, -k)
+        arrive(origin, full, k - 1)
+        if k < 4:
+            push(out_ref.at[origin], origin, full, right, k)
+        push(out_ref.at[origin], origin, head, across, 15 + k)
+        if k < 4:
+            origin = at(col, k)
+            arrive(origin, full, 3 + k)
+            if k < 3:
+                push(out_ref.at[origin], origin, full, left, 4 + k)
+            push(out_ref.at[origin], origin, head, across, 19 + k)
+        origin = at(other, -k)
+        arrive(origin, tail, 6 + k)
+        if k < 4:
+            push(out_ref.at[origin], origin, tail, right, 7 + k)
+        if k < 4:
+            origin = at(other, k)
+            arrive(origin, tail, 10 + k)
+            if k < 3:
+                push(out_ref.at[origin], origin, tail, left, 11 + k)
+    arrive(across, head, 15)
+    for k in range(1, 5):
+        arrive(at(other, -k), head, 15 + k)
+        if k < 4:
+            arrive(at(other, k), head, 19 + k)
+    keep.wait()
+    for copy in sends:
+        copy.wait_send()
+
+
+def gather_tokens(tokens):
+    rows, width = tokens.shape
+    out = pl.pallas_call(
+        gather_kernel,
+        out_shape=jax.ShapeDtypeStruct((2 * ZN, rows, width), tokens.dtype),
+        in_specs=[pl.BlockSpec(memory_space=pltpu.VMEM)],
+        out_specs=pl.BlockSpec(memory_space=pl.ANY),
+        scratch_shapes=[
+            pltpu.SemaphoreType.DMA,
+            pltpu.SemaphoreType.DMA((23,)),
+            pltpu.SemaphoreType.DMA((23,)),
+        ],
+        cost_estimate=pl.CostEstimate(flops=0, transcendentals=0, bytes_accessed=200000000),
+        compiler_params=pltpu.CompilerParams(collective_id=0, has_side_effects=True),
+    )(tokens)
+    return out.reshape(2 * ZN * rows, width)
+
+
+def sum_kernel(x_ref, out_ref, slots, send_sem, recv_sem):
+    count = 2 * ZN
+    tp = lax.axis_index("tp")
+    peers = [lax.rem(tp + d, count) for d in range(1, count)]
+    greet(peers)
+    copies = []
+    for d in range(1, count):
+        copy = pltpu.make_async_remote_copy(
+            src_ref=x_ref,
+            dst_ref=slots.at[d],
+            send_sem=send_sem.at[d],
+            recv_sem=recv_sem.at[d],
+            device_id={"tp": peers[d - 1]},
+            device_id_type=MESH,
+        )
+        copy.start()
+        copies.append(copy)
+    for copy in copies:
+        copy.wait()
+    total = x_ref[...]
+    for d in range(1, count):
+        total = total + slots[d]
+    out_ref[...] = total
+
+
+def sum_over_tp(x):
+    return pl.pallas_call(
+        sum_kernel,
+        out_shape=jax.ShapeDtypeStruct(x.shape, x.dtype),
+        in_specs=[pl.BlockSpec(memory_space=pltpu.VMEM)],
+        out_specs=pl.BlockSpec(memory_space=pltpu.VMEM),
+        scratch_shapes=[
+            pltpu.VMEM((2 * ZN,) + x.shape, x.dtype),
+            pltpu.SemaphoreType.DMA((2 * ZN,)),
+            pltpu.SemaphoreType.DMA((2 * ZN,)),
+        ],
+        cost_estimate=pl.CostEstimate(flops=0, transcendentals=0, bytes_accessed=20000000),
+        compiler_params=pltpu.CompilerParams(collective_id=1, has_side_effects=True),
+    )(x)
 
 
 def token_layout(lengths_row, prefix_row, block_len):
@@ -78,11 +234,13 @@
     offsets = jnp.arange(page_span, dtype=jnp.int32)
     source = start_of[:, None] + offsets[None, :]
     is_valid = offsets[None, :] < length_of[:, None]
-    source = jnp.clip(source, 0, kv_new.shape[0] - 1).reshape(-1)
-    taken_rows = jnp.take(kv_new, source, axis=0).reshape(
-        owner_count, page_span, kv_new.shape[1], kv_new.shape[2]
-    )
-    return jnp.where(is_valid[:, :, None, None], taken_rows, jnp.zeros_like(taken_rows))
+    source = jnp.where(is_valid, source, -1).reshape(-1)
+    block_len = kv_new.shape[0]
+    pick = (source[:, None] == jnp.arange(block_len, dtype=jnp.int32)[None, :]).astype(kv_new.dtype)
+    flat = jnp.dot(
+        pick, kv_new.reshape(block_len, -1), preferred_element_type=jnp.float32
+    ).astype(kv_new.dtype)
+    return flat.reshape(owner_count, page_span, kv_new.shape[1], kv_new.shape[2])
 
 
 def hand_over(kv_new, lengths_row, starts_at, owner_row):
@@ -105,10 +263,10 @@
 ):
     local_width = qkv_weight.shape[2]
     heads_here = local_width // HEAD
-    block_tokens = lax.all_gather(tokens, "tp", axis=0, tiled=True)
+    block_tokens = gather_tokens(tokens)
     block_len = block_tokens.shape[0]
-    row_piece = lax.all_gather(qkv_weight, "req", axis=0, tiled=True)
-    flat_piece = row_piece.reshape(row_piece.shape[0], 3 * local_width)
+    flat_rows = qkv_weight.reshape(qkv_weight.shape[0], 3 * local_width)
+    flat_piece = lax.all_gather(flat_rows, "req", axis=0, tiled=True)
     joined_all = jnp.dot(block_tokens, flat_piece, preferred_element_type=jnp.float32)
     joined_all = joined_all.reshape(block_len, 3, local_width)
     queries = joined_all[:, 0]
@@ -117,7 +275,7 @@
     local_sums = jnp.stack(
         [jnp.sum(queries * queries, axis=1), jnp.sum(keys_raw * keys_raw, axis=1)]
     )
-    global_sums = lax.psum(local_sums, "tp")
+    global_sums = sum_over_tp(local_sums)
     inverse = lax.rsqrt(global_sums / (HEADS * HEAD) + norm_eps)
     queries = queries * inverse[0][:, None] * query_key_gain[0]
     keys_raw = keys_raw * inverse[1][:, None] * query_key_gain[1]

time: 492 us -> 435 us (0.88)
  waiting for transfers between devices: 143 us -> 0.73 us
  Pallas kernels: 0 us -> 107 us
  local copies, waits for them, and re-layouts: 95.2 us -> 70.2 us
  other arithmetic: 43.9 us -> 34.5 us
  matrix products: 58.6 us -> 65.1 us
  blocking collectives: 136 us -> 142 us
    all_gather x2 -> x1, waiting for transfers between devices: 141 us -> 0.01 us  [body(): flat_piece = lax.all_gather(flat_rows, 'req', axis=0, tiled=True)]
    pallas_call x0 -> x2, Pallas kernels: none -> 107 us  [the longest x1 96.2 us: gather_tokens(): pl.pallas_call(gather_kernel, out_shape=jax.ShapeDtypeStruct((2 * ZN, row...]
    all_to_all x1, blocking collectives: 109 us -> 142 us  [hand_over(): lax.all_to_all(outgoing, 'req', split_axis=0, concat_axis=0, tiled=True)]
    gather x1 -> x0, local copies, waits for them, and re-layouts: 32.4 us -> none  [build_send(): jnp.take(kv_new, source, axis=0)]
    psum x1 -> x0, blocking collectives: 26.2 us -> none  [body(): global_sums = lax.psum(local_sums, 'tp')]
    select_n x2 -> x0, other arithmetic: 12.7 us -> none  [the longest x1 12.7 us: build_send(): jnp.where(is_valid[:, :, None, None], taken_rows, jnp.zeros_like(taken_ro...]
    all_gather x1 -> x0, local copies, waits for them, and re-layouts: 10.8 us -> none  [body(): row_piece = lax.all_gather(qkv_weight, 'req', axis=0, tiled=True)]
    dot_general x0 -> x1, local copies, waits for them, and re-layouts: none -> 10.7 us  [body(): jnp.dot(block_tokens, flat_piece, preferred_element_type=jnp.float32)]
  transfers between devices with their start and end apart: 4 -> 3, of which waited for: 2 -> 0; matrix products, arithmetic and copies ran while one was open for 36% -> 33% of each run, Pallas kernels for 0% -> 25%
where the time goes in v1:
time: 435 us; the launch traced here: 434 us
  blocking collectives  142 us (33%)
  Pallas kernels  107 us (25%)
  local copies, waits for them, and re-layouts  70.2 us (16%)
  matrix products  65.1 us (15%)
  other arithmetic  34.5 us (8%)
  between operations  14 us (3%)
    all_to_all x1, blocking collectives, hand_over(): lax.all_to_all(outgoing, 'req', split_axis=0, concat_axis=0, tiled=True)  142 us
    pallas_call x1, Pallas kernels, gather_tokens(): pl.pallas_call(gather_kernel, out_shape=jax.ShapeDtypeStruct((2 * ZN, row...  96.2 us
    slice x1, local copies, waits for them, and re-layouts, body(): pool_cache[:, :, 1, :].reshape(pool_count * PAGE, heads_here, HEAD)  21.7 us
    dot_general x2, matrix products, attend_head(): jnp.dot(queries, pool_keys.T, preferred_element_type=jnp.float32)  18.5 us
    reduce_sum x4, other arithmetic, attend_head(): row_total = jnp.sum(pool_exp, axis=1) + jnp.sum(block_exp, axis=1)  18.3 us
    unnamed x36, local copies, waits for them, and re-layouts  15.7 us
    dot_general x2, matrix products, attend_head(): jnp.dot(pool_weights, pool_values, preferred_element_type=jnp.float32)  15.6 us
    dot_general x1, matrix products, body(): jnp.dot(block_tokens, flat_piece, preferred_element_type=jnp.float32)  12 us
  transfers between devices with their start and end apart: 3, of which 0 were waited for; matrix products, arithmetic and copies ran while one was open for 33% of the time, Pallas kernels for 25%

profile of v1, /device:TPU:1, one launch (start us, length us, event | category | flops | bytes accessed | tf_op | source)
XLA Modules:
  0.0 433.6 jit_solution(3281941059842709681)
XLA Ops:
  7.2 1.3 copy.44
  8.5 1.0 copy.45
  9.6 0.7 all-gather.5.cloned.1.call-update
  10.5 96.2 %shard_map.113 = bf16[16,56,5120]{2,1,0:T(8,128)(2,1)} custom-call(bf16[56,5120]{1,0:T(8,128)(2,1)} %tok_ref.1), custom_call_target="tpu_custom_call" | custom-call | bytes 200000000 | tf_op jit(solution)/shard_map/pallas_call | solution.py:116
  107.0 0.6 fusion.39
  107.7 21.7 %slice_reduce_fusion = (bf16[32,128,256]{2,1,0:T(8,128)(2,1)}, bf16[32,128,256]{2,1,0:T(8,128)(2,1)}) fusion(bf16[32,128,2,256]{3,2,1,0:T(2,128)(2,1)} %param.17), kind=kLoop, calls=%fused_computation.43 | loop fusion | bytes 8388608 | tf_op jit(solution)/shard_map/slice | solution.py:303
  129.4 2.6 reshape.228
  132.0 4.0 reshape.227
  136.5 1.7 multiply_cosine_fusion
  138.1 4.2 copy_bitcast_fusion
  142.3 10.7 %copy.46 = bf16[768,5120]{1,0:T(8,128)(2,1)} copy(bf16[768,5120]{0,1:T(8,128)(2,1)} %bitcast.96) | data formatting | bytes 15728640 | tf_op jit(solution)/shard_map/dot_general | solution.py:270
  153.0 12.0 %fusion.42 = f32[896,3,256]{0,2,1:T(8,128)S(1)} fusion(bf16[896,5120,1]{1,0,2:T(8,128)(2,1)} %bitcast.95, bf16[3,256,5120]{2,1,0:T(8,128)(2,1)} %bitcast.97), kind=kOutput, calls=%fused_computation.93 | convolution fusion | flops 7046430720 | bytes 19791872 | tf_op jit(solution)/shard_map/dot_general | solution.py:270
  165.1 1.1 multiply_reduce_fusion.1
  166.2 2.6 copy.50
  168.8 0.6 pad_maximum_fusion.1.x_ref
  169.4 10.3 %shard_map.114 = f32[2,896]{1,0:T(2,128)} custom-call(f32[2,896]{1,0:T(2,128)} %pad_maximum_fusion.1.x_ref), custom_call_target="tpu_custom_call" | custom-call | bytes 20000000 | tf_op jit(solution)/shard_map/pallas_call | solution.py:158
  179.8 0.7 add_rsqrt_fusion
  180.5 1.2 copy.47
  181.7 1.8 multiply_multiply_fusion
  183.5 1.3 subtract_convert_fusion
  184.8 0.4 multiply_subtract_fusion
  185.3 1.0 copy.52
  186.3 2.3 maximum_bitcast_fusion
  188.6 1.0 fusion.48
  189.6 59.7 %while.12 = (s32[]{:T(128)}, bf16[2,896,128]{1,2,0:T(8,128)(2,1)}, bf16[2,896,128]{2,1,0:T(8,128)(2,1)}, bf16[2,4096,128]{2,1,0:T(8,128)(2,1)}, bf16[2,896,128]{...) while((s32[]{:T(128)}, bf16[2,896,128]{1,2,0:T(8,128)(2,1)}, ...), condition=%wide.region_13.14_spmd.clone.clone, body=%wide.region_8.13_spmd.clone.clone.sunk | while | flops 2354198784 | bytes 64388300 | solution.py:304
  189.8 9.2 %fusion.59 = (f32[896]{0:T(1024)S(1)}, f32[896,4096]{1,0:T(8,128)}) fusion(s32[4096]{0:T(1024)S(1)} %get-tuple-element.262, s32[896]{0:T(1024)S(1)} %get-tuple-element.263, bf16[2,4096,128]{2,1,0:T(8,128)(2,1)} %get-tuple-element.258, s32[]{:T(128)S(6)} %copy.72, bf16[2,896,128]{2,1,0:T(8,128)(2,1)} %get-tuple-element.257), kind=kOutput, calls=%fused_computation.6.clone.1 | convolution fusion | flops 954203264 | bytes 15982592 | tf_op jit(solution)/shard_map/while/body/eval_jaxpr/dot_general | solution.py:212
  199.1 1.7 fusion.60
  200.8 8.6 %fusion.61 = f32[896]{0:T(1024)S(1)} fusion(f32[896,4096]{1,0:T(8,128)} %get-tuple-element.231, s32[4096]{0:T(1024)S(1)} %get-tuple-element.262, f32[896]{0:T(1024)S(1)} %max.10, s32[896]{0:T(1024)S(1)} %get-tuple-element.263), kind=kLoop, calls=%fused_computation.5.clone.1 | loop fusion | flops 18349184 | bytes 14707200 | tf_op jit(solution)/shard_map/while/body/eval_jaxpr/reduce_sum | solution.py:219
  209.5 0.5 fusion.62
  210.0 7.8 %fusion.63 = f32[896,128]{1,0:T(8,128)S(1)} fusion(f32[896,4096]{1,0:T(8,128)} %get-tuple-element.231, s32[4096]{0:T(1024)S(1)} %get-tuple-element.262, f32[896]{0:T(1024)S(1)} %add.109, f32[896]{0:T(1024)S(1)} %max.10, s32[896]{0:T(1024)S(1)} %get-tuple-element.263, bf16[2,4096,128]{2,1,0:T(8,128)(2,1)S(1)} %get-tuple-element.260, s32[]{:T(128)S(6)} %copy.72), kind=kOutput, calls=%fused_computation.7.clone.1 | convolution fusion | flops 961544192 | bytes 16216068 | tf_op jit(solution)/shard_map/while/body/eval_jaxpr/dot_general | solution.py:222
  217.8 0.7 fusion.64
  218.8 0.8 copy-done.9
  219.6 9.2 %fusion.59 = (f32[896]{0:T(1024)S(1)}, f32[896,4096]{1,0:T(8,128)}) fusion(s32[4096]{0:T(1024)S(1)} %get-tuple-element.262, s32[896]{0:T(1024)S(1)} %get-tuple-element.263, bf16[2,4096,128]{2,1,0:T(8,128)(2,1)} %get-tuple-element.258, s32[]{:T(128)S(6)} %copy.72, bf16[2,896,128]{2,1,0:T(8,128)(2,1)} %get-tuple-element.257), kind=kOutput, calls=%fused_computation.6.clone.1 | convolution fusion | flops 954203264 | bytes 15982592 | tf_op jit(solution)/shard_map/while/body/eval_jaxpr/dot_general | solution.py:212
  228.8 1.7 fusion.60
  230.5 8.6 %fusion.61 = f32[896]{0:T(1024)S(1)} fusion(f32[896,4096]{1,0:T(8,128)} %get-tuple-element.231, s32[4096]{0:T(1024)S(1)} %get-tuple-element.262, f32[896]{0:T(1024)S(1)} %max.10, s32[896]{0:T(1024)S(1)} %get-tuple-element.263), kind=kLoop, calls=%fused_computation.5.clone.1 | loop fusion | flops 18349184 | bytes 14707200 | tf_op jit(solution)/shard_map/while/body/eval_jaxpr/reduce_sum | solution.py:219
  239.2 0.5 fusion.62
  239.7 7.8 %fusion.63 = f32[896,128]{1,0:T(8,128)S(1)} fusion(f32[896,4096]{1,0:T(8,128)} %get-tuple-element.231, s32[4096]{0:T(1024)S(1)} %get-tuple-element.262, f32[896]{0:T(1024)S(1)} %add.109, f32[896]{0:T(1024)S(1)} %max.10, s32[896]{0:T(1024)S(1)} %get-tuple-element.263, bf16[2,4096,128]{2,1,0:T(8,128)(2,1)S(1)} %get-tuple-element.260, s32[]{:T(128)S(6)} %copy.72), kind=kOutput, calls=%fused_computation.7.clone.1 | convolution fusion | flops 961544192 | bytes 16216068 | tf_op jit(solution)/shard_map/while/body/eval_jaxpr/dot_general | solution.py:222
  247.5 0.7 fusion.64
  248.6 0.8 copy-done.9
  249.3 8.0 %convolution_convert_fusion = bf16[896,5120]{1,0:T(8,128)(2,1)} fusion(bf16[896,256]{0,1:T(8,128)(2,1)} %bitcast.104, bf16[256,5120]{0,1:T(8,128)(2,1)} %all-gather.5.cloned.1.call-done), kind=kOutput, calls=%fused_computation.40 | convolution fusion | flops 2353397760 | bytes 12255232 | tf_op jit(solution)/shard_map/dot_general | solution.py:319
  257.4 0.6 copy-done.13
  258.5 0.3 maximum_convert_fusion
  259.2 6.2 %fusion.34 = bf16[4096,512]{1,0:T(8,128)(2,1)} fusion(bf16[896,512]{0,1:T(8,128)(2,1)S(1)} %bitcast.103, s32[4096]{0:T(1024)S(1)} %bitcast.106), kind=kOutput, calls=%fused_computation.42 | convolution fusion | flops 3763863552 | bytes 5128192 | tf_op jit(solution)/shard_map/dot_general | solution.py:240
  265.3 7.0 %reshape.224 = bf16[16,256,2,256]{3,2,1,0:T(2,128)(2,1)} reshape(bf16[4096,512]{1,0:T(8,128)(2,1)} %fusion.34) | data formatting | bytes 8388608 | tf_op jit(solution)/shard_map/reshape | solution.py:243
  272.3 142.1 %all_to_all.5 = bf16[16,256,2,256]{3,2,1,0:T(2,128)(2,1)} all-to-all(bf16[16,256,2,256]{3,2,1,0:T(2,128)(2,1)} %reshape.224), channel_id=1, replica_groups=mesh['req'=16,'tp'=16] {'req'}, dimensions={0} | all-to-all | bytes 8388608 | tf_op jit(solution)/shard_map/all_to_all | solution.py:248
  414.4 1.3 fusion.35
  415.7 2.1 fusion.38
  417.9 9.2 %copy.79 = bf16[32,128,2,256]{3,2,1,0:T(2,128)(2,1)} copy(bf16[32,128,2,256]{3,2,1,0:T(2,128)(2,1)} %bitcast.94) | data formatting | bytes 8388608
  (82 shorter events, 2.8 us)
Async XLA Ops:
  7.2 135.1 %all-gather.3.cloned.1.call-start = ((), (), s32[]{:S(2)}) async-start(), calls=%async_computation.2 | async-start | bytes 8355840 | tf_op jit(solution)/shard_map/all_gather | solution.py:269
  9.6 239.7 %all-gather.5.cloned.1.call-start = ((), (), s32[]{:S(2)}) async-start(), calls=%async_computation.3 | async-start | bytes 2785280 | tf_op jit(solution)/shard_map/all_gather | solution.py:317
  10.3 404.1 %reduce-scatter.2.cloned.1.call-start = ((), (), s32[]{:S(2)}) async-start(), calls=%async_computation.4 | async-start | bytes 9748480 | tf_op jit(solution)/shard_map/reduce_scatter | solution.py:318
  10.4 96.2 %copy-start.16 = (f32[2,256]{1,0:T(2,128)S(1)}, f32[2,256]{1,0:T(2,128)}, u32[]{:S(2)}) copy-start(f32[2,256]{1,0:T(2,128)} %param.15) | copy-start | bytes 6148
  10.4 96.2 %copy-start.12 = (s32[1,16]{1,0:T(1,128)S(1)}, s32[1,16]{1,0:T(1,128)}, u32[]{:S(2)}) copy-start(s32[1,16]{1,0:T(1,128)} %param.18) | copy-start | bytes 196
  10.4 96.6 %copy-start.14 = (s32[1,16]{1,0:T(1,128)S(1)}, s32[1,16]{1,0:T(1,128)}, u32[]{:S(2)}) copy-start(s32[1,16]{1,0:T(1,128)} %param.19) | copy-start | bytes 196
  129.4 6.9 %copy-start.18 = (s32[1,32]{1,0:T(1,128)S(1)}, s32[1,32]{1,0:T(1,128)}, u32[]{:S(2)}) copy-start(s32[1,32]{1,0:T(1,128)} %param.20) | copy-start | bytes 388
  166.2 19.1 %copy-start = (bf16[896,1,256]{0,2,1:T(8,128)(2,1)}, bf16[896,1,256]{0,2,1:T(8,128)(2,1)S(1)}, u32[]{:S(2)}) copy-start(bf16[896,1,256]{0,2,1:T(8,128)(2,1)S(1)} %slice.76) | copy-start | bytes 1376260
  185.3 4.4 %copy-start.2 = (bf16[896,2,64]{2,0,1:T(8,128)(2,1)}, bf16[896,2,64]{2,0,1:T(8,128)(2,1)S(1)}, u32[]{:S(2)}) copy-start(bf16[896,2,64]{2,0,1:T(8,128)(2,1)S(1)} %get-tuple-element.158) | copy-start | bytes 688132
  185.3 4.4 %copy-start.4 = (bf16[896,2,64]{2,0,1:T(8,128)(2,1)}, bf16[896,2,64]{2,0,1:T(8,128)(2,1)S(1)}, u32[]{:S(2)}) copy-start(bf16[896,2,64]{2,0,1:T(8,128)(2,1)S(1)} %get-tuple-element.159) | copy-start | bytes 688132
  185.3 4.4 %copy-start.7 = (bf16[2,4096,128]{2,1,0:T(8,128)(2,1)S(1)}, bf16[2,4096,128]{2,1,0:T(8,128)(2,1)}, u32[]{:S(2)}) copy-start(bf16[2,4096,128]{2,1,0:T(8,128)(2,1)} %get-tuple-element.240) | copy-start | bytes 6291460
  210.0 7.8 %copy-start.10 = (bf16[2,896,128]{2,1,0:T(8,128)(2,1)S(1)}, bf16[2,896,128]{2,1,0:T(8,128)(2,1)}, u32[]{:S(2)}) copy-start(bf16[2,896,128]{2,1,0:T(8,128)(2,1)} %get-tuple-element.261) | copy-start | bytes 1376260 | tf_op jit(solution)/shard_map/while
  217.8 1.0 copy-start.8
  218.8 0.8 copy-start.9
  239.7 7.8 %copy-start.10 = (bf16[2,896,128]{2,1,0:T(8,128)(2,1)S(1)}, bf16[2,896,128]{2,1,0:T(8,128)(2,1)}, u32[]{:S(2)}) copy-start(bf16[2,896,128]{2,1,0:T(8,128)(2,1)} %get-tuple-element.261) | copy-start | bytes 1376260 | tf_op jit(solution)/shard_map/while
  247.5 1.0 copy-start.8
  248.5 0.8 copy-start.9
  257.3 0.7 copy-start.13
  257.3 0.7 copy-start.15
  257.3 0.7 copy-start.17
  257.3 1.0 copy-start.3
  257.4 1.2 copy-start.5
  257.4 1.7 copy-start.1
  272.3 143.4 %copy-start.6 = (bf16[56,5120]{1,0:T(8,128)(2,1)S(1)}, bf16[56,5120]{1,0:T(8,128)(2,1)}, u32[]{:S(2)}) copy-start(bf16[56,5120]{1,0:T(8,128)(2,1)} %tok_ref.1) | copy-start | bytes 1720324
  272.3 143.4 %copy-start.11 = (f32[5120]{0:T(1024)S(1)}, f32[5120]{0:T(1024)}, u32[]{:S(2)}) copy-start(f32[5120]{0:T(1024)} %param.16) | copy-start | bytes 61444
Sparse Core Ops, SparseCore 0:
  11.3 103.5 all-gather.2
  117.6 52.5 all-gather.4
  257.5 144.9 reduce-scatter.1
